TPU v7x, 32 devices: a whole 2x2x4 slice. The times are simulated.
32 devices in a mesh: tgt: 8 (over z, core), sup: 4 (over y, x).
Axes of the slice: x: 2, y: 2, z: 4, core: 2. Of those that a mesh axis runs over, the one named last changes fastest.
Arguments:
- target_pool: float32 [512, 3, 1024], P('tgt'), may hold values from -6 to 6
- target_index: int32 [64], P('tgt'), may hold values from 0 to 511, as said below
- target_labels: int32 [64], P('tgt'), may hold values from 0 to 99
- dual_weights: float32 [128, 100], P('sup'), may hold values from -0.5 to 0.5
- support_images: float32 [128, 3, 1024], P(('sup', 'tgt')), may hold values from -6 to 6
Outputs:
- residual: float32 [64, 100], P('tgt')
- support_grad: float32 [128, 3, 1024], P(('sup', 'tgt'))
Inputs may be any that keep to these rules, and one draw needn't show every extreme that they name: `target_index`: for each j, the targets 8 * j to 8 * (j + 1) - 1 name distinct candidates among 64 * j to 64 * (j + 1) - 1.
All inputs are finite; a program needn't handle non-finite values.
Results may differ from a plain program's by a relative error of at most 0.0003.
Values sent between devices are 32-bit elements; how exact they have to be, the bound alone decides.
A program may use at most 64 MiB of HBM per device.

v0:
```python
import math
import jax
import jax.numpy as jnp
from jax import lax
from jax.sharding import PartitionSpec as P

CHANNELS = 3
SIDE = 32
CLASSES = 100
LAYERS = 3
PIXELS = 1024
bias_variance = 0.01


def box_filter(pixel_map):
    column = jnp.arange(PIXELS) % SIDE
    zero_column = jnp.zeros(pixel_map.shape[:-1] + (1,), pixel_map.dtype)
    shifted_right = jnp.concatenate([zero_column, pixel_map[..., :-1]], axis=-1)
    shifted_left = jnp.concatenate([pixel_map[..., 1:], zero_column], axis=-1)
    across = (
        pixel_map
        + jnp.where(column > 0, shifted_right, 0.0)
        + jnp.where(column < SIDE - 1, shifted_left, 0.0)
    )
    zero_row = jnp.zeros(pixel_map.shape[:-1] + (SIDE,), pixel_map.dtype)
    shifted_down = jnp.concatenate([zero_row, across[..., :-SIDE]], axis=-1)
    shifted_up = jnp.concatenate([across[..., SIDE:], zero_row], axis=-1)
    return (across + shifted_down + shifted_up) / 9.0


def self_maps(images):
    energy = images[:, 0] * images[:, 0]
    for channel in range(1, CHANNELS):
        energy = energy + images[:, channel] * images[:, channel]
    current = box_filter(energy / CHANNELS) + bias_variance
    levels = [current]
    for layer_index in range(1, LAYERS):
        current = box_filter(current) + bias_variance
        levels.append(current)
    return levels


def rectified(cross, target_level, support_level):
    spread = jnp.sqrt(target_level * support_level - cross * cross)
    polar_angle = jnp.arctan2(spread, cross)
    return ((spread + (math.pi - polar_angle) * cross) / math.pi, spread, polar_angle)


def cross_forward(targets, support, target_levels, support_levels):
    inner_sum = targets[:, None, 0] * support[None, :, 0]
    for channel in range(1, CHANNELS):
        inner_sum = inner_sum + targets[:, None, channel] * support[None, :, channel]
    cross = box_filter(inner_sum / CHANNELS) + bias_variance
    saved_maps = []
    output_map = cross
    for layer_index in range(LAYERS):
        output_map, spread, polar_angle = rectified(
            cross, target_levels[layer_index][:, None], support_levels[layer_index][None]
        )
        saved_maps.append((spread, polar_angle))
        if layer_index + 1 < LAYERS:
            cross = box_filter(output_map) + bias_variance
    return (jnp.mean(output_map, axis=-1), saved_maps)


def cross_backward(weight, saved_maps, targets, support, support_levels):
    upstream = weight[:, :, None]
    level_grad = None
    for layer_index in range(LAYERS - 1, -1, -1):
        spread, polar_angle = saved_maps[layer_index]
        level_term = jnp.sum(upstream * spread, axis=0) / (
            2.0 * math.pi * support_levels[layer_index]
        )
        level_grad = level_term if level_grad is None else level_term + box_filter(level_grad)
        upstream = box_filter(upstream * (math.pi - polar_angle) / math.pi)
    energy_grad = box_filter(level_grad) / CHANNELS
    channel_grads = []
    for channel in range(CHANNELS):
        carried = jnp.sum(upstream * targets[:, None, channel], axis=0) / CHANNELS
        channel_grads.append(carried + 2.0 * support[:, channel] * energy_grad)
    return jnp.stack(channel_grads, axis=1)


def shards(target_pool, target_index, target_labels, dual_weights, support_images):
    local_rows = target_index - lax.axis_index("tgt") * target_pool.shape[0]
    targets = jnp.take(target_pool, local_rows, axis=0)
    onehot = (target_labels[:, None] == jnp.arange(CLASSES)[None, :]).astype(jnp.float32)
    own_count = support_images.shape[0]
    all_targets, all_onehot = (
        lax.all_gather(targets, "tgt", axis=0, tiled=True),
        lax.all_gather(onehot, "tgt", axis=0, tiled=True),
    )
    own_duals = lax.dynamic_slice_in_dim(
        dual_weights, lax.axis_index("tgt") * own_count, own_count, 0
    )
    support_levels = self_maps(support_images)
    kernel, saved_maps = cross_forward(
        all_targets, support_images, self_maps(all_targets), support_levels
    )
    partial_value = jnp.dot(
        kernel, own_duals, precision=lax.Precision.HIGHEST, preferred_element_type=jnp.float32
    )
    predicted = lax.psum(partial_value, ("tgt", "sup"))
    residual_all = predicted - all_onehot
    weight = jnp.dot(
        residual_all,
        own_duals.T,
        precision=lax.Precision.HIGHEST,
        preferred_element_type=jnp.float32,
    )
    support_grad = cross_backward(weight, saved_maps, all_targets, support_images, support_levels)
    residual = lax.dynamic_slice_in_dim(
        residual_all, lax.axis_index("tgt") * targets.shape[0], targets.shape[0], 0
    )
    return (residual, support_grad)


def solution(mesh):
    in_specs = (
        P("tgt", None, None),
        P("tgt"),
        P("tgt"),
        P("sup", None),
        P(("sup", "tgt"), None, None),
    )
    out_specs = (P("tgt", None), P(("sup", "tgt"), None, None))
    return jax.shard_map(shards, mesh=mesh, in_specs=in_specs, out_specs=out_specs, check_vma=False)
```

profile of v0, /device:TPU:0, one launch (start us, length us, event | category | flops | bytes accessed | tf_op | source)
XLA Modules:
  0.0 109.1 jit_solution(5623943175997622236)
XLA Ops:
  0.7 0.7 copy-done.9
  1.8 0.7 gather_fusion
  2.6 17.2 %all_gather.6 = f32[64,3,1024]{2,0,1:T(8,128)S(1)} all-gather(f32[8,3,1024]{2,0,1:T(8,128)S(1)} %broadcast_select_fusion), channel_id=1, replica_groups=mesh['tgt'=8,'sup'=4] {'tgt'}, dimensions={0}, use_global_device_ids=true | all-gather | bytes 884736 | tf_op jit(solution)/shard_map/all_gather | solution.py:90
  19.8 0.9 broadcast_multiply_fusion.1
  21.3 0.7 copy-done.6
  22.3 0.4 fusion.26
  22.7 0.5 select_add_fusion.5
  23.9 2.3 %add_multiply_fusion.3 = (f32[64,4,1024]{2,0,1:T(8,128)S(1)}, f32[64,4,1024]{2,0,1:T(8,128)S(1)}) fusion(f32[4,1024]{1,0:T(4,128)S(1)} %multiply_add_fusion.10, f32[64,1024]{1,0:T(8,128)S(1)} %multiply_add_fusion.5, f32[64,4,992]{2,0,1:T(8,128)S(1)} %get-tuple-element.42, f32[64,4,1024]{2,0,1:T(8,128)S(1)} %select_add_fusion.5, ...), kind=kLoop, calls=%fused_computation.26 | loop fusion | flops 2883584 | bytes 5455872 | tf_op jit(solution)/shard_map/div | solution.py:46
  26.2 0.4 fusion.24
  26.6 0.5 select_add_fusion.4
  28.3 3.2 %add_multiply_fusion.2 = (f32[64,4,1024]{2,0,1:T(8,128)S(1)}, f32[64,4,1024]{2,0,1:T(8,128)}) fusion(f32[4,1024]{1,0:T(4,128)S(1)} %multiply_add_fusion.9, f32[64,1024]{1,0:T(8,128)S(1)} %multiply_add_fusion.4, f32[64,4,992]{2,0,1:T(8,128)S(1)} %get-tuple-element.38, f32[64,4,1024]{2,0,1:T(8,128)S(1)} %select_add_fusion.4, ...), kind=kLoop, calls=%fused_computation.21 | loop fusion | flops 2883584 | bytes 5455872 | tf_op jit(solution)/shard_map/div | solution.py:46
  31.5 0.4 fusion.22
  31.9 0.4 select_add_fusion.3
  33.7 2.7 %multiply_reduce_fusion.6 = (f32[64,4]{0,1:T(4,128)S(1)}, f32[64,4,1024]{2,0,1:T(8,128)S(1)}) fusion(f32[4,1024]{1,0:T(4,128)S(1)} %multiply_add_fusion.8, f32[64,1024]{1,0:T(8,128)S(1)} %multiply_add_fusion.3, f32[64,4,992]{2,0,1:T(8,128)S(1)} %get-tuple-element.34, f32[64,4,1024]{2,0,1:T(8,128)S(1)} %select_add_fusion.3, ...), kind=kLoop, calls=%fused_computation.16 | loop fusion | flops 3145472 | bytes 4408320 | tf_op jit(solution)/shard_map/reduce_sum | solution.py:63
  36.4 0.9 fusion.6
  37.3 40.9 %psum.7 = f32[64,100]{1,0:T(8,128)} all-reduce(f32[64,100]{1,0:T(8,128)S(1)} %fusion.6), channel_id=1, replica_groups=mesh['tgt'=8,'sup'=4] {'tgt','sup'}, use_global_device_ids=true, to_apply=%region_1.2 | all-reduce | flops 6400 | bytes 51200 | tf_op jit(solution)/shard_map/psum | solution.py:103
  78.3 14.2 %all_gather.7 = f32[64,100]{1,0:T(8,128)S(1)} all-gather(f32[8,100]{1,0:T(8,128)S(1)} %fusion.5), channel_id=1, replica_groups=mesh['tgt'=8,'sup'=4] {'tgt'}, dimensions={0}, use_global_device_ids=true | all-gather | bytes 28800 | tf_op jit(solution)/shard_map/all_gather | solution.py:91
  92.5 0.8 fusion.8
  93.4 3.1 %multiply_reduce_fusion.2 = (f32[4,1024]{1,0:T(4,128)S(1)}, f32[64,4,1024]{2,0,1:T(8,128)S(1)}) fusion(f32[64,4,1024]{2,0,1:T(8,128)S(1)} %get-tuple-element.8, f32[64,4]{0,1:T(4,128)S(1)} %fusion.8, f32[4,1024]{1,0:T(4,128)S(1)} %multiply_add_fusion.8, f32[64,1024]{1,0:T(8,128)} %copy-done.2), kind=kLoop, calls=%fused_computation.3 | loop fusion | flops 2093056 | bytes 2393088 | tf_op jit(solution)/shard_map/reduce_sum | solution.py:71
  96.7 0.4 fusion.20
  97.1 0.4 select_add_fusion.2
  97.9 0.8 copy-done.1
  98.7 2.3 %multiply_reduce_fusion.3 = (f32[4,1024]{1,0:T(4,128)S(1)}, f32[64,4,1024]{2,0,1:T(8,128)S(1)}) fusion(f32[64,4,1024]{2,0,1:T(8,128)S(1)} %copy-done.1, f32[4,1024]{1,0:T(4,128)S(1)} %multiply_add_fusion.9, f32[64,1024]{1,0:T(8,128)S(1)} %multiply_add_fusion.4, f32[64,4,992]{2,0,1:T(8,128)S(1)} %get-tuple-element.30, f32[64,4,1024]{2,0,1:T(8,128)S(1)} %select_add_fusion.2, ...), kind=kLoop, calls=%fused_computation.4 | loop fusion | flops 2879488 | bytes 5472256 | tf_op jit(solution)/shard_map/reduce_sum | solution.py:71
  101.4 0.4 fusion.18
  101.8 0.4 select_add_fusion.1
  102.6 2.3 %multiply_reduce_fusion.4 = (f32[4,1024]{1,0:T(4,128)S(1)}, f32[64,4,1024]{2,0,1:T(8,128)S(1)}) fusion(f32[64,4,1024]{2,0,1:T(8,128)S(1)} %get-tuple-element.12, f32[4,1024]{1,0:T(4,128)S(1)} %multiply_add_fusion.10, f32[64,1024]{1,0:T(8,128)S(1)} %multiply_add_fusion.5, f32[64,4,992]{2,0,1:T(8,128)S(1)} %get-tuple-element.26, ...), kind=kLoop, calls=%fused_computation.5 | loop fusion | flops 2879488 | bytes 5472256 | tf_op jit(solution)/shard_map/reduce_sum | solution.py:71
  105.2 0.4 fusion.16
  105.6 0.4 select_add_fusion
  106.5 0.5 copy-done.3
  107.2 0.5 multiply_reduce_fusion.5
  107.9 0.6 pad_maximum_fusion
  108.5 0.6 constant_dynamic-slice_fusion
  (70 shorter events, 6.9 us)
Async XLA Ops:
  0.6 1.2 %copy-start = (f32[64,3,1024]{2,0,1:T(8,128)S(1)}, f32[64,3,1024]{2,0,1:T(8,128)}, u32[]{:S(2)}) copy-start(f32[64,3,1024]{2,0,1:T(8,128)} %param.5) | copy-start | bytes 2359300
  0.7 0.7 copy-start.9
  21.3 0.8 copy-start.6
  33.4 3.0 %copy-start.2 = (f32[64,1024]{1,0:T(8,128)}, f32[64,1024]{1,0:T(8,128)S(1)}, u32[]{:S(2)}) copy-start(f32[64,1024]{1,0:T(8,128)S(1)} %multiply_add_fusion.3) | copy-start | bytes 786436
  37.3 40.9 %copy-start.8 = (s32[8]{0:T(128)S(1)}, s32[8]{0:T(128)}, u32[]{:S(2)}) copy-start(s32[8]{0:T(128)} %param.7) | copy-start | bytes 100
  78.2 14.3 %copy-start.7 = (f32[64,100]{1,0:T(8,128)S(1)}, f32[64,100]{1,0:T(8,128)}, u32[]{:S(2)}) copy-start(f32[64,100]{1,0:T(8,128)} %psum.7) | copy-start | bytes 76804
  97.5 1.2 %copy-start.1 = (f32[64,4,1024]{2,0,1:T(8,128)S(1)}, f32[64,4,1024]{2,0,1:T(8,128)}, u32[]{:S(2)}) copy-start(f32[64,4,1024]{2,0,1:T(8,128)} %get-tuple-element.10) | copy-start | bytes 3145732
  106.1 1.0 copy-start.3
  106.1 1.0 copy-start.4
  106.1 1.1 %copy-start.5 = (f32[64,1024]{1,0:T(8,128)S(1)}, f32[64,1024]{1,0:T(8,128)}, u32[]{:S(2)}) copy-start(f32[64,1024]{1,0:T(8,128)} %get-tuple-element.48) | copy-start | bytes 786436
where the time goes:
time: 110 us; the launch traced here: 109 us
  blocking collectives  72.3 us (66%)
  other arithmetic  22.9 us (21%)
  local copies, waits for them, and re-layouts  11.1 us (10%)
  matrix products  1.75 us (2%)
    psum x1, blocking collectives, shards(): predicted = lax.psum(partial_value, ('tgt', 'sup'))  40.9 us
    all_gather x1, blocking collectives, shards(): lax.all_gather(targets, 'tgt', axis=0, tiled=True)  17.2 us
    all_gather x1, blocking collectives, shards(): lax.all_gather(onehot, 'tgt', axis=0, tiled=True)  14.2 us
    reduce_sum x3, other arithmetic, cross_backward(): jnp.sum(upstream * spread, axis=0)  7.66 us
    div x2, other arithmetic, rectified(): (spread + (math.pi - polar_angle) * cross) / math.pi  5.48 us
    add x15, other arithmetic, box_filter(): pixel_map + jnp.where(column > 0, shifted_right, 0.0)  3.66 us
    unnamed x20, local copies, waits for them, and re-layouts  3.37 us
    slice x15, local copies, waits for them, and re-layouts, box_filter(): shifted_right = jnp.concatenate([zero_column, pixel_map[..., :-1]], axis=-1)  3.19 us

commit v1 on v0

--- a/solution.py
+++ b/solution.py
@@ -3,6 +3,7 @@
 import jax.numpy as jnp
 from jax import lax
 from jax.sharding import PartitionSpec as P
+from jax.lax import all_gather
 
 CHANNELS = 3
 SIDE = 32
@@ -100,7 +101,8 @@
     partial_value = jnp.dot(
         kernel, own_duals, precision=lax.Precision.HIGHEST, preferred_element_type=jnp.float32
     )
-    predicted = lax.psum(partial_value, ("tgt", "sup"))
+    work_series_all = lambda patch: jnp.sum(all_gather(patch, ("tgt", "sup")), 0)
+    predicted = work_series_all(partial_value)
     residual_all = predicted - all_onehot
     weight = jnp.dot(
         residual_all,

time: 110 us -> 145 us (1.32)
  blocking collectives: 72.3 us -> 106 us
    all_gather x0 -> x1, blocking collectives: none -> 74.4 us  [shards(): all_gather(patch, ('tgt', 'sup'))]
    psum x1 -> x0, blocking collectives: 40.9 us -> none  [shards(): predicted = lax.psum(partial_value, ('tgt', 'sup'))]
where the time goes in v1:
time: 145 us
  blocking collectives  106 us (73%)
  other arithmetic  23.9 us (16%)
  local copies, waits for them, and re-layouts  12.4 us (9%)
  matrix products  1.75 us (1%)
    all_gather x1, blocking collectives, shards(): all_gather(patch, ('tgt', 'sup'))  74.4 us
    all_gather x1, blocking collectives, shards(): lax.all_gather(targets, 'tgt', axis=0, tiled=True)  17.2 us
    all_gather x1, blocking collectives, shards(): lax.all_gather(onehot, 'tgt', axis=0, tiled=True)  14.1 us
    reduce_sum x3, other arithmetic, cross_backward(): jnp.sum(upstream * spread, axis=0)  7.66 us
    div x2, other arithmetic, rectified(): (spread + (math.pi - polar_angle) * cross) / math.pi  6.39 us
    unnamed x20, local copies, waits for them, and re-layouts  4.76 us
    add x15, other arithmetic, box_filter(): pixel_map + jnp.where(column > 0, shifted_right, 0.0)  3.65 us
    slice x15, local copies, waits for them, and re-layouts, box_filter(): shifted_right = jnp.concatenate([zero_column, pixel_map[..., :-1]], axis=-1)  3.19 us

profile of v1, /device:TPU:0, one launch (start us, length us, event | category | flops | bytes accessed | tf_op | source)
XLA Modules:
  0.0 144.8 jit_solution(15433403463688709808)
XLA Ops:
  0.7 0.7 copy-done.9
  1.8 0.7 gather_fusion
  2.6 17.2 %all_gather.12 = f32[64,3,1024]{2,0,1:T(8,128)S(1)} all-gather(f32[8,3,1024]{2,0,1:T(8,128)S(1)} %broadcast_select_fusion), channel_id=1, replica_groups=mesh['tgt'=8,'sup'=4] {'tgt'}, dimensions={0}, use_global_device_ids=true | all-gather | bytes 884736 | tf_op jit(solution)/shard_map/all_gather | solution.py:91
  19.8 0.9 broadcast_multiply_fusion.1
  21.3 0.7 copy-done.7
  22.7 0.5 select_add_fusion.5
  23.9 3.2 %add_multiply_fusion.3 = (f32[64,4,1024]{2,0,1:T(8,128)S(1)}, f32[64,4,1024]{2,0,1:T(8,128)}) fusion(f32[4,1024]{1,0:T(4,128)S(1)} %multiply_add_fusion.10, f32[64,1024]{1,0:T(8,128)S(1)} %multiply_add_fusion.5, f32[64,4,992]{2,0,1:T(8,128)S(1)} %get-tuple-element.42, f32[64,4,1024]{2,0,1:T(8,128)S(1)} %select_add_fusion.5, ...), kind=kLoop, calls=%fused_computation.26 | loop fusion | flops 2883584 | bytes 5455872 | tf_op jit(solution)/shard_map/div | solution.py:47
  27.5 0.5 select_add_fusion.4
  29.3 3.2 %add_multiply_fusion.2 = (f32[64,4,1024]{2,0,1:T(8,128)S(1)}, f32[64,4,1024]{2,0,1:T(8,128)}) fusion(f32[4,1024]{1,0:T(4,128)S(1)} %multiply_add_fusion.9, f32[64,1024]{1,0:T(8,128)S(1)} %multiply_add_fusion.4, f32[64,4,992]{2,0,1:T(8,128)S(1)} %get-tuple-element.38, f32[64,4,1024]{2,0,1:T(8,128)S(1)} %select_add_fusion.4, ...), kind=kLoop, calls=%fused_computation.21 | loop fusion | flops 2883584 | bytes 5455872 | tf_op jit(solution)/shard_map/div | solution.py:47
  32.5 0.4 fusion.22
  32.9 0.4 select_add_fusion.3
  34.6 2.7 %multiply_reduce_fusion.6 = (f32[64,4]{0,1:T(4,128)S(1)}, f32[64,4,1024]{2,0,1:T(8,128)S(1)}) fusion(f32[4,1024]{1,0:T(4,128)S(1)} %multiply_add_fusion.8, f32[64,1024]{1,0:T(8,128)S(1)} %multiply_add_fusion.3, f32[64,4,992]{2,0,1:T(8,128)S(1)} %get-tuple-element.34, f32[64,4,1024]{2,0,1:T(8,128)S(1)} %select_add_fusion.3, ...), kind=kLoop, calls=%fused_computation.16 | loop fusion | flops 3145472 | bytes 4408320 | tf_op jit(solution)/shard_map/reduce_sum | solution.py:64
  37.3 0.9 fusion.6
  38.2 74.4 %all-gather = f32[2048,100]{1,0:T(8,128)S(1)} all-gather(f32[64,100]{1,0:T(8,128)S(1)} %fusion.6), channel_id=2, replica_groups=mesh['tgt'=8,'sup'=4] {'tgt','sup'}, dimensions={0}, use_global_device_ids=true | all-gather | bytes 844800 | tf_op jit(solution)/shard_map/all_gather | solution.py:104
  112.7 0.6 copy-done.8
  113.3 14.1 %all_gather.15 = f32[64,100]{1,0:T(8,128)S(1)} all-gather(f32[8,100]{1,0:T(8,128)S(1)} %fusion.5), channel_id=1, replica_groups=mesh['tgt'=8,'sup'=4] {'tgt'}, dimensions={0}, use_global_device_ids=true | all-gather | bytes 28800 | tf_op jit(solution)/shard_map/all_gather | solution.py:92
  127.4 0.8 fusion.8
  128.2 3.1 %multiply_reduce_fusion.2 = (f32[4,1024]{1,0:T(4,128)S(1)}, f32[64,4,1024]{2,0,1:T(8,128)S(1)}) fusion(f32[64,4,1024]{2,0,1:T(8,128)S(1)} %get-tuple-element.8, f32[64,4]{0,1:T(4,128)S(1)} %fusion.8, f32[4,1024]{1,0:T(4,128)S(1)} %multiply_add_fusion.8, f32[64,1024]{1,0:T(8,128)} %copy-done.3), kind=kLoop, calls=%fused_computation.3 | loop fusion | flops 2093056 | bytes 2393088 | tf_op jit(solution)/shard_map/reduce_sum | solution.py:72
  131.6 0.4 fusion.20
  132.0 0.4 select_add_fusion.2
  132.8 0.8 copy-done.2
  133.6 2.3 %multiply_reduce_fusion.3 = (f32[4,1024]{1,0:T(4,128)S(1)}, f32[64,4,1024]{2,0,1:T(8,128)S(1)}) fusion(f32[64,4,1024]{2,0,1:T(8,128)S(1)} %copy-done.2, f32[4,1024]{1,0:T(4,128)S(1)} %multiply_add_fusion.9, f32[64,1024]{1,0:T(8,128)S(1)} %multiply_add_fusion.4, f32[64,4,992]{2,0,1:T(8,128)S(1)} %get-tuple-element.30, f32[64,4,1024]{2,0,1:T(8,128)S(1)} %select_add_fusion.2, ...), kind=kLoop, calls=%fused_computation.4 | loop fusion | flops 2879488 | bytes 5472256 | tf_op jit(solution)/shard_map/reduce_sum | solution.py:72
  136.2 0.4 fusion.18
  136.7 0.4 select_add_fusion.1
  137.5 0.8 copy-done.1
  138.3 2.3 %multiply_reduce_fusion.4 = (f32[4,1024]{1,0:T(4,128)S(1)}, f32[64,4,1024]{2,0,1:T(8,128)S(1)}) fusion(f32[64,4,1024]{2,0,1:T(8,128)S(1)} %copy-done.1, f32[4,1024]{1,0:T(4,128)S(1)} %multiply_add_fusion.10, f32[64,1024]{1,0:T(8,128)S(1)} %multiply_add_fusion.5, f32[64,4,992]{2,0,1:T(8,128)S(1)} %get-tuple-element.26, ...), kind=kLoop, calls=%fused_computation.5 | loop fusion | flops 2879488 | bytes 5472256 | tf_op jit(solution)/shard_map/reduce_sum | solution.py:72
  141.0 0.4 fusion.16
  141.4 0.4 select_add_fusion
  142.2 0.5 copy-done.4
  142.9 0.5 multiply_reduce_fusion.5
  143.6 0.6 pad_maximum_fusion
  144.2 0.6 constant_dynamic-slice_fusion
  (71 shorter events, 7.8 us)
Async XLA Ops:
  0.6 1.2 copy-start
  0.7 0.7 copy-start.9
  21.3 0.8 copy-start.7
  34.3 3.0 %copy-start.3 = (f32[64,1024]{1,0:T(8,128)}, f32[64,1024]{1,0:T(8,128)S(1)}, u32[]{:S(2)}) copy-start(f32[64,1024]{1,0:T(8,128)S(1)} %multiply_add_fusion.3) | copy-start | bytes 786436
  112.6 0.7 copy-start.8
  132.4 1.2 copy-start.2
  137.1 1.2 copy-start.1
  141.8 1.0 copy-start.4
  141.8 1.0 copy-start.5
  141.8 1.1 copy-start.6
